TPU v7x, 32 devices: a whole 2x2x4 slice. The times are simulated.
32 devices in a mesh: pipe: 4 (over y, x), expert: 8 (over z, core).
Axes of the slice: x: 2, y: 2, z: 4, core: 2. Of those that a mesh axis runs over, the one named last changes fastest.
Arguments:
- activations: bfloat16 [4, 1024, 2560], P('pipe', 'expert'), may hold values from -6 to 6
- out_grad: bfloat16 [4, 1024, 2560], P('pipe', 'expert'), may hold values from -6 to 6
- expert_ids: int32 [4, 1024, 2], P('pipe', 'expert'), may hold values from 0 to 3, all different within a row; in each aligned block of 128 rows (0 to 127, 128 to 255, ..., all dimensions but the last counted through in order) at most 96 rows name the same one
- gate_values: float32 [4, 1024, 2], P('pipe', 'expert'), may hold values from 0.1 to 1
- w_gate: bfloat16 [4, 2560, 3072], P('pipe', None, 'expert'), may hold values from -0.125 to 0.125
- w_up: bfloat16 [4, 2560, 3072], P('pipe', None, 'expert'), may hold values from -0.125 to 0.125
- w_down: bfloat16 [4, 3072, 2560], P('pipe', 'expert'), may hold values from -0.21875 to 0.21875
Outputs:
- passed_grad: bfloat16 [4, 1024, 2560], P('pipe', 'expert')
- router_grad: float32 [4, 1024, 2], P('pipe', 'expert')
Inputs may be any that keep to these rules, and one draw needn't show every extreme that they name: `expert_ids`: each row names 2 different experts. In the 128 rows of one section on one device (aligned blocks of rows) no expert is named by more than 96 rows, a bound that some block reaches; every expert is named somewhere.
All inputs are finite; a program needn't handle non-finite values.
Results may differ from a plain program's by a relative error of at most 0.0095.
Values may be sent and summed in bfloat16 or wider, within the bound.
A program may use at most 128 MiB of HBM per device.

v0:
```python
import jax
import jax.numpy as jnp
from jax import lax
from jax.sharding import PartitionSpec as P


def shifted(block, axis, distance):
    devices = range(lax.axis_size(axis))
    route = [(i - distance, i) for i in devices if i - distance in devices]
    return lax.ppermute(block, axis, route)


def expert_terms(rows_in, rows_grad, gate_cols, up_cols, down_rows):
    contract = (((1,), (1,)), ((), ()))
    gate_pre = jnp.dot(rows_in, gate_cols, preferred_element_type=jnp.float32)
    up_pre = jnp.dot(rows_in, up_cols, preferred_element_type=jnp.float32)
    squash = jax.nn.sigmoid(gate_pre)
    activated = gate_pre * squash
    hidden = (activated * up_pre).astype(jnp.bfloat16)
    back_hidden = lax.dot_general(
        rows_grad, down_rows, contract, preferred_element_type=jnp.float32
    )
    router_part = jnp.sum(hidden.astype(jnp.float32) * back_hidden, axis=1)
    slope = squash * (1.0 + gate_pre * (1.0 - squash))
    grad_gate = (back_hidden * up_pre * slope).astype(jnp.bfloat16)
    grad_up = (back_hidden * activated).astype(jnp.bfloat16)
    route_part = lax.dot_general(grad_gate, gate_cols, contract, preferred_element_type=jnp.float32)
    route_part = route_part + lax.dot_general(
        grad_up, up_cols, contract, preferred_element_type=jnp.float32
    )
    return (route_part, router_part)


def local(activations, out_grad, expert_ids, gate_values, w_gate, w_up, w_down):
    inputs = activations[0]
    grads_out = out_grad[0]
    routes = expert_ids[0]
    weights_gate = gate_values[0]
    gate_local = w_gate[0]
    up_local = w_up[0]
    down_local = w_down[0]
    devices_e = lax.axis_size("expert")
    owners = devices_e // 2
    tokens_dev, top_k = routes.shape
    feat_width = inputs.shape[1]
    capacity = min(tokens_dev * 3 // 4, tokens_dev * top_k * 3 // (2 * owners))
    count_entries = tokens_dev * top_k
    flat_ids = routes.reshape(-1)
    one_hot = (flat_ids[:, None] == jnp.arange(owners, dtype=jnp.int32)[None, :]).astype(jnp.int32)
    slot_rank = jnp.sum((jnp.cumsum(one_hot, axis=0) - 1) * one_hot, axis=1)
    slot_index = flat_ids * capacity + slot_rank
    slot_table = (
        jnp.full((owners * capacity,), count_entries, jnp.int32)
        .at[slot_index]
        .set(jnp.arange(count_entries, dtype=jnp.int32))
    )
    token_of = slot_table // top_k
    pad_row = jnp.zeros((1, feat_width), inputs.dtype)
    send_in = jnp.concatenate([inputs, pad_row], 0)[token_of].reshape(owners, capacity, feat_width)
    send_grad = jnp.concatenate([grads_out, pad_row], 0)[token_of].reshape(
        owners, capacity, feat_width
    )
    full_in = lax.all_to_all(
        jnp.repeat(send_in, 2, axis=0), "expert", split_axis=0, concat_axis=0, tiled=True
    )
    item_count = full_in.shape[1]
    route_part, router_part = expert_terms(
        full_in.reshape(-1, feat_width),
        lax.all_to_all(
            jnp.repeat(send_grad, 2, axis=0), "expert", split_axis=0, concat_axis=0, tiled=True
        ).reshape(-1, feat_width),
        gate_local,
        up_local,
        down_local,
    )
    route_part = route_part.reshape(devices_e, item_count, feat_width)
    router_part = router_part.reshape(devices_e, item_count)
    back_route = lax.all_to_all(
        route_part.astype(jnp.bfloat16), "expert", split_axis=0, concat_axis=0, tiled=True
    ).astype(route_part.dtype)
    back_router = lax.all_to_all(
        router_part.astype(jnp.bfloat16), "expert", split_axis=0, concat_axis=0, tiled=True
    ).astype(router_part.dtype)
    summed = jnp.sum(back_route.reshape(owners, 2, item_count, feat_width), axis=1)
    router_sum = jnp.sum(back_router.reshape(owners, 2, item_count), axis=1)
    route_sum, router_sum = (summed, router_sum)
    entry_route = route_sum.reshape(-1, feat_width)[slot_index]
    entry_router = router_sum.reshape(-1)[slot_index]
    input_grad = jnp.sum(
        weights_gate.reshape(tokens_dev, top_k, 1)
        * entry_route.reshape(tokens_dev, top_k, feat_width),
        axis=1,
    ).astype(jnp.bfloat16)
    passed = shifted(input_grad, "pipe", -1)
    return (passed[None], entry_router.reshape(tokens_dev, top_k)[None])


def solution(mesh):
    return jax.shard_map(
        local,
        mesh=mesh,
        in_specs=(
            P("pipe", "expert", None),
            P("pipe", "expert", None),
            P("pipe", "expert", None),
            P("pipe", "expert", None),
            P("pipe", None, "expert"),
            P("pipe", None, "expert"),
            P("pipe", "expert", None),
        ),
        out_specs=(P("pipe", "expert", None), P("pipe", "expert", None)),
        check_vma=False,
    )
```

profile of v0, /device:TPU:1, one launch (start us, length us, event | category | flops | bytes accessed | tf_op | source)
XLA Modules:
  0.0 348.9 jit_solution(5297020244395157370)
XLA Ops:
  0.6 0.9 copy.21
  1.7 0.1 eq.25
  1.9 0.7 broadcast_multiply_fusion
  2.5 1.2 reduce-window.6
  4.3 0.1 mul.57
  4.4 1.4 scatter_custom_fusion
  5.9 1.1 concatenate.7
  7.0 3.3 gather_fusion.1
  10.3 3.8 %broadcast_in_dim.24 = bf16[4,2,96,2560]{3,2,1,0:T(8,128)(2,1)} broadcast(bf16[4,96,2560]{2,1,0:T(8,128)(2,1)} %bitcast.56), dimensions={0,2,3} | broadcast | bytes 5898240 | tf_op jit(solution)/shard_map/broadcast_in_dim | solution.py:64
  14.1 6.5 %all-to-all-start.1 = ((bf16[8,96,2560]{2,1,0:T(8,128)(2,1)}), bf16[8,96,2560]{2,1,0:T(8,128)(2,1)}, u32[]{:S(2)}, u32[]{:S(2)}) async-start(bf16[8,96,2560]{2,1,0:T(8,128)(2,1)} %bitcast.52), calls=%async_computation.1 | async-start | bytes 7864320 | tf_op jit(solution)/shard_map/all_to_all | solution.py:63
  20.6 3.3 gather_fusion
  23.9 84.2 %all-to-all-done.1 = bf16[8,96,2560]{2,1,0:T(8,128)(2,1)} async-done(((bf16[8,96,2560]{2,1,0:T(8,128)(2,1)}), bf16[8,96,2560]{2,1,0:T(8,128)(2,1)}, u32[]{:S(2)}, u32[]{:S(2)}) %all-to-all-start.1) | async-done | bytes 3932192 | tf_op jit(solution)/shard_map/all_to_all | solution.py:63
  108.1 3.8 %broadcast_in_dim.23 = bf16[4,2,96,2560]{3,2,1,0:T(8,128)(2,1)} broadcast(bf16[4,96,2560]{2,1,0:T(8,128)(2,1)} %bitcast.55), dimensions={0,2,3} | broadcast | bytes 5898240 | tf_op jit(solution)/shard_map/broadcast_in_dim | solution.py:70
  111.9 5.4 %all-to-all-start = ((bf16[8,96,2560]{2,1,0:T(8,128)(2,1)}), bf16[8,96,2560]{2,1,0:T(8,128)(2,1)}, u32[]{:S(2)}, u32[]{:S(2)}) async-start(bf16[8,96,2560]{2,1,0:T(8,128)(2,1)} %bitcast.53), calls=%async_computation | async-start | bytes 7864320 | tf_op jit(solution)/shard_map/all_to_all | solution.py:69
  117.3 4.0 %fusion.2 = f32[768,384]{0,1:T(8,128)S(1)} fusion(bf16[768,2560]{1,0:T(8,128)(2,1)} %bitcast.13, bf16[1,2560,384]{2,1,0:T(8,128)(2,1)S(1)} %copy-done), kind=kOutput, calls=%fused_computation.10 | convolution fusion | flops 1509949440 | bytes 7077888 | tf_op jit(solution)/shard_map/dot_general | solution.py:15
  121.3 4.9 %fusion.5 = f32[768,384]{0,1:T(8,128)} fusion(bf16[768,2560]{1,0:T(8,128)(2,1)} %bitcast.13, bf16[1,2560,384]{2,1,0:T(8,128)(2,1)S(1)} %copy-done.2), kind=kOutput, calls=%fused_computation.13 | convolution fusion | flops 1509949440 | bytes 7077888 | tf_op jit(solution)/shard_map/dot_general | solution.py:16
  126.1 78.6 %all-to-all-done = bf16[8,96,2560]{2,1,0:T(8,128)(2,1)} async-done(((bf16[8,96,2560]{2,1,0:T(8,128)(2,1)}), bf16[8,96,2560]{2,1,0:T(8,128)(2,1)}, u32[]{:S(2)}, u32[]{:S(2)}) %all-to-all-start) | async-done | bytes 3932192 | tf_op jit(solution)/shard_map/all_to_all | solution.py:69
  204.8 4.9 %multiply_reduce_fusion.1 = (bf16[768]{0:T(1024)(128)(2,1)S(1)}, f32[768,384]{0,1:T(8,128)S(1)}) fusion(f32[768,384]{0,1:T(8,128)} %fusion.5, f32[768,384]{0,1:T(8,128)S(1)} %fusion.2, bf16[768,2560]{1,0:T(8,128)(2,1)} %bitcast.8, bf16[1,384,2560]{2,1,0:T(8,128)(2,1)} %param.13), kind=kOutput, calls=%fused_computation.17 | convolution fusion | flops 1512602880 | bytes 9438720 | tf_op jit(solution)/shard_map/dot_general | solution.py:20
  209.7 2.5 fusion
  212.2 4.3 %add_convert_fusion = bf16[768,2560]{1,0:T(8,128)(2,1)} fusion(f32[768,2560]{1,0:T(8,128)S(1)} %fusion, bf16[1,2560,384]{2,1,0:T(8,128)(2,1)S(1)} %copy-done.3, f32[768,384]{0,1:T(8,128)S(1)} %get-tuple-element.7, f32[768,384]{0,1:T(8,128)S(1)} %fusion.2), kind=kOutput, calls=%fused_computation.6 | convolution fusion | flops 1515651072 | bytes 16121856 | tf_op jit(solution)/shard_map/dot_general | solution.py:28
  216.5 5.5 %all-to-all-start.2 = ((bf16[8,96,2560]{2,1,0:T(8,128)(2,1)}), bf16[8,96,2560]{2,1,0:T(8,128)(2,1)}, u32[]{:S(2)}, u32[]{:S(2)}) async-start(bf16[8,96,2560]{2,1,0:T(8,128)(2,1)} %bitcast.54), calls=%async_computation.2 | async-start | bytes 7864320 | tf_op jit(solution)/shard_map/all_to_all | solution.py:78
  222.1 87.4 %all-to-all-done.2 = bf16[8,96,2560]{2,1,0:T(8,128)(2,1)} async-done(((bf16[8,96,2560]{2,1,0:T(8,128)(2,1)}), bf16[8,96,2560]{2,1,0:T(8,128)(2,1)}, u32[]{:S(2)}, u32[]{:S(2)}) %all-to-all-start.2) | async-done | bytes 3932192 | tf_op jit(solution)/shard_map/all_to_all | solution.py:78
  309.5 5.2 %convert_reduce_fusion = f32[4,96,2560]{2,1,0:T(8,128)} fusion(bf16[8,96,2560]{2,1,0:T(8,128)(2,1)} %all-to-all-done.2), kind=kLoop, calls=%fused_computation.5 | loop fusion | flops 2949120 | bytes 7864320 | tf_op jit(solution)/shard_map/reduce_sum | solution.py:84
  314.7 6.2 %gather_fusion.2 = f32[256,2560]{1,0:T(8,128)} fusion(f32[384,2560]{1,0:T(8,128)} %bitcast.51, s32[1024]{0:T(1024)S(1)} %pad_clamp_fusion), kind=kCustom, calls=%fused_computation.2 | custom fusion | bytes 5243904 | tf_op jit(solution)/shard_map/gather | solution.py:87
  320.9 4.4 %reshape.115 = f32[128,2,2560]{2,1,0:T(2,128)} reshape(f32[256,2560]{1,0:T(8,128)} %gather_fusion.2) | data formatting | bytes 5242880 | tf_op jit(solution)/shard_map/reshape | solution.py:91
  325.3 5.5 %multiply_reduce_fusion = bf16[128,2560]{1,0:T(8,128)(2,1)S(1)} fusion(f32[128,2,2560]{2,1,0:T(2,128)} %reshape.115, f32[128,2]{1,0:T(8,128)S(1)} %copy.19), kind=kLoop, calls=%fused_computation.7 | loop fusion | flops 983040 | bytes 3277824 | tf_op jit(solution)/shard_map/reduce_sum | solution.py:89
  330.8 1.3 collective-permute-start
  332.2 8.2 %all_to_all.21 = bf16[8,1,96]{2,1,0:T(2,128)(2,1)S(1)} all-to-all(bf16[8,1,96]{2,1,0:T(2,128)(2,1)S(1)} %convert_element_type.64), channel_id=1, replica_groups=mesh['pipe'=4,'expert'=8] {'expert'}, dimensions={0} | all-to-all | bytes 3072 | tf_op jit(solution)/shard_map/all_to_all | solution.py:81
  340.5 1.9 gather_fusion.3
  342.6 0.6 copy.26
  343.3 4.8 %collective-permute-done = bf16[128,2560]{1,0:T(8,128)(2,1)S(1)} collective-permute-done((bf16[128,2560]{1,0:T(8,128)(2,1)S(1)}, bf16[128,2560]{1,0:T(8,128)(2,1)S(1)}, u32[]{:S(2)}, u32[]{:S(2)}) %collective-permute-start) | collective-permute-done | bytes 655392 | tf_op jit(solution)/shard_map/ppermute | solution.py:10
  348.1 0.8 copy.30
  (34 shorter events, 1.2 us)
Async XLA Ops:
  0.6 116.6 %copy-start = (bf16[1,2560,384]{2,1,0:T(8,128)(2,1)S(1)}, bf16[1,2560,384]{2,1,0:T(8,128)(2,1)}, u32[]{:S(2)}) copy-start(bf16[1,2560,384]{2,1,0:T(8,128)(2,1)} %param.11) | copy-start | bytes 5898244
  14.1 6.5 %copy-start.4 = (bf16[1,128,2560]{2,1,0:T(8,128)(2,1)S(1)}, bf16[1,128,2560]{2,1,0:T(8,128)(2,1)}, u32[]{:S(2)}) copy-start(bf16[1,128,2560]{2,1,0:T(8,128)(2,1)} %param.8) | copy-start | bytes 1966084
  14.1 94.0 %all-to-all-start.1 = ((bf16[8,96,2560]{2,1,0:T(8,128)(2,1)}), bf16[8,96,2560]{2,1,0:T(8,128)(2,1)}, u32[]{:S(2)}, u32[]{:S(2)}) async-start(bf16[8,96,2560]{2,1,0:T(8,128)(2,1)} %bitcast.52), calls=%async_computation.1 | async-start | bytes 7864320 | tf_op jit(solution)/shard_map/all_to_all | solution.py:63
  111.9 92.9 %all-to-all-start = ((bf16[8,96,2560]{2,1,0:T(8,128)(2,1)}), bf16[8,96,2560]{2,1,0:T(8,128)(2,1)}, u32[]{:S(2)}, u32[]{:S(2)}) async-start(bf16[8,96,2560]{2,1,0:T(8,128)(2,1)} %bitcast.53), calls=%async_computation | async-start | bytes 7864320 | tf_op jit(solution)/shard_map/all_to_all | solution.py:69
  117.3 4.0 %copy-start.2 = (bf16[1,2560,384]{2,1,0:T(8,128)(2,1)S(1)}, bf16[1,2560,384]{2,1,0:T(8,128)(2,1)}, u32[]{:S(2)}) copy-start(bf16[1,2560,384]{2,1,0:T(8,128)(2,1)} %param.12) | copy-start | bytes 5898244
  204.8 4.9 %copy-start.1 = (f32[768,384]{0,1:T(8,128)S(1)}, f32[768,384]{0,1:T(8,128)}, u32[]{:S(2)}) copy-start(f32[768,384]{0,1:T(8,128)} %fusion.5) | copy-start | bytes 3538948
  209.7 2.5 copy-start.3
  216.5 5.5 %copy-start.5 = (f32[1,128,2]{1,2,0:T(2,128)S(1)}, f32[1,128,2]{1,2,0:T(2,128)}, u32[]{:S(2)}) copy-start(f32[1,128,2]{1,2,0:T(2,128)} %param.10) | copy-start | bytes 3076
  216.5 93.0 %all-to-all-start.2 = ((bf16[8,96,2560]{2,1,0:T(8,128)(2,1)}), bf16[8,96,2560]{2,1,0:T(8,128)(2,1)}, u32[]{:S(2)}, u32[]{:S(2)}) async-start(bf16[8,96,2560]{2,1,0:T(8,128)(2,1)} %bitcast.54), calls=%async_computation.2 | async-start | bytes 7864320 | tf_op jit(solution)/shard_map/all_to_all | solution.py:78
  330.8 17.2 %collective-permute-start = (bf16[128,2560]{1,0:T(8,128)(2,1)S(1)}, bf16[128,2560]{1,0:T(8,128)(2,1)S(1)}, u32[]{:S(2)}, u32[]{:S(2)}) collective-permute-start(bf16[128,2560]{1,0:T(8,128)(2,1)S(1)} %multiply_reduce_fusion), channel_id=1, source_target_pairs={{8,0},{16,8},{24,16},{9,1},{17,9},{25,17},{10,2},{18,10},{26,18},{... | collective-permute-start | bytes 1966088 | tf_op jit(solution)/shard_map/ppermute | solution.py:10
where the time goes:
time: 351 us; the launch traced here: 349 us
  waiting for transfers between devices  255 us (73%)
  local copies, waits for them, and re-layouts  32.9 us (9%)
  matrix products  20.5 us (6%)
  starting transfers between devices  18.7 us (5%)
  other arithmetic  12.8 us (4%)
  blocking collectives  8.21 us (2%)
    all_to_all x1, waiting for transfers between devices, local(): lax.all_to_all(route_part.astype(jnp.bfloat16), 'expert', split_axis=0, c...  87.4 us
    all_to_all x1, waiting for transfers between devices, local(): lax.all_to_all(jnp.repeat(send_in, 2, axis=0), 'expert', split_axis=0, co...  84.2 us
    all_to_all x1, waiting for transfers between devices, local(): lax.all_to_all(jnp.repeat(send_grad, 2, axis=0), 'expert', split_axis=0,...  78.6 us
    all_to_all x1, blocking collectives, local(): lax.all_to_all(router_part.astype(jnp.bfloat16), 'expert', split_axis=0,...  8.21 us
  transfers between devices with their start and end apart: 4, of which 4 were waited for; matrix products, arithmetic and copies ran while one was open for 4% of the time, Pallas kernels for 0%

commit v1 on v0

--- a/solution.py
+++ b/solution.py
@@ -1,6 +1,10 @@
+import functools
+
 import jax
 import jax.numpy as jnp
 from jax import lax
+from jax.experimental import pallas as pl
+from jax.experimental.pallas import tpu as pltpu
 from jax.sharding import PartitionSpec as P
 
 
@@ -31,7 +35,7 @@
     return (route_part, router_part)
 
 
-def local(activations, out_grad, expert_ids, gate_values, w_gate, w_up, w_down):
+def routed_local(activations, out_grad, expert_ids, gate_values, w_gate, w_up, w_down):
     inputs = activations[0]
     grads_out = out_grad[0]
     routes = expert_ids[0]
@@ -95,6 +99,532 @@
     return (passed[None], entry_router.reshape(tokens_dev, top_k)[None])
 
 
+MESH = pl.DeviceIdType.MESH
+NT = (((1,), (1,)), ((), ()))
+
+
+def line_kernel(
+    n, cap, sx_ref, sg_ref, wt_ref, pt_ref, wg_hbm, wu_hbm, wd_hbm, out_ref, rr_ref,
+    xa, ga, xb, gb, xo, go, wgu, wd, wp, pre, gs, gr, part, ca, cb, ta, tb, fin, wts, pts, rl, rs,
+    w_sem, o_ssem, rn_sem, a_ssem, a_psem, ra_sem, b_ssem, b_psem, rb_sem, wt_ssem, wt_rsem,
+    pt_ssem, pt_rsem, wp_ssem, wp_rsem, g_ssem, g_rsem, ca_ssem, ca_rsem, cb_ssem, cb_rsem,
+    rr_ssem, rr_rsem, f_ssem, f_rsem,
+):
+    stage = lax.axis_index("pipe")
+    me = lax.axis_index("expert")
+    stages = lax.axis_size("pipe")
+    c, k = lax.div(me, 2), lax.rem(me, 2)
+    other = 1 - k
+    tok = sx_ref.shape[1]
+    rest = tok - cap
+    hid = wd.shape[0]
+    half_d = wp.shape[0]
+    partner = (stage, c * 2 + other)
+    send, land_a, land_b, land_o = (sx_ref, sg_ref), (xa, ga), (xb, gb), (xo, go)
+
+    def rdma(src, dst, ssem, rsem, dev):
+        return pltpu.make_async_remote_copy(
+            src_ref=src, dst_ref=dst, send_sem=ssem, recv_sem=rsem, device_id=dev, device_id_type=MESH
+        )
+
+    loads = [
+        pltpu.make_async_copy(wg_hbm, wgu.at[:, pl.ds(0, hid)], w_sem.at[0]),
+        pltpu.make_async_copy(wu_hbm, wgu.at[:, pl.ds(hid, hid)], w_sem.at[1]),
+        pltpu.make_async_copy(wd_hbm, wd, w_sem.at[2]),
+    ]
+    for load in loads:
+        load.start()
+    rl[...] = jnp.zeros_like(rl)
+
+    barrier = pltpu.get_barrier_semaphore()
+    for j in range(1, 2 * n):
+        pl.semaphore_signal(barrier, inc=1, device_id=(stage, lax.rem(me + j, 2 * n)), device_id_type=MESH)
+    for kk in range(2):
+
+        @pl.when(stage > 0)
+        def _():
+            pl.semaphore_signal(barrier, inc=1, device_id=(stage - 1, c * 2 + kk), device_id_type=MESH)
+
+        @pl.when(stage < stages - 1)
+        def _():
+            pl.semaphore_signal(barrier, inc=1, device_id=(stage + 1, c * 2 + kk), device_id_type=MESH)
+
+    near = (stage > 0).astype(jnp.int32) + (stage < stages - 1).astype(jnp.int32)
+    pl.semaphore_wait(barrier, 2 * n - 1 + 2 * near)
+
+    def mirrored(s, chip):
+        return chip if s == 0 else n - 1 - chip
+
+    def onward(s):
+        return (stage, (c + 1 - 2 * s) * 2 + k)
+
+    def backward(s):
+        return (stage, (c - 1 + 2 * s) * 2 + k)
+
+    def own_a(s, h):
+        return rdma(send[h].at[s, pl.ds(0, cap)], land_a[h].at[c, pl.ds(k * cap, cap)],
+                    a_ssem.at[s, c, h], ra_sem.at[me, h], onward(s))
+
+    def fwd_a(s, t, h):
+        view = land_a[h].at[t, pl.ds(k * cap, cap)]
+        return rdma(view, view, a_ssem.at[s, t, h], ra_sem.at[t * 2 + k, h], onward(s))
+
+    def pair_a(t, h):
+        view = land_a[h].at[t, pl.ds(k * cap, cap)]
+        return rdma(view, view, a_psem.at[t, h], ra_sem.at[t * 2 + k, h], partner)
+
+    def got_a(t, kk, h):
+        view = land_a[h].at[t, pl.ds(kk * cap, cap)]
+        return rdma(view, view, a_psem.at[t, h], ra_sem.at[t * 2 + kk, h], partner)
+
+    def own_b(s, h):
+        return rdma(send[h].at[s, pl.ds(cap, rest)], land_b[h].at[c, pl.ds(k * rest, rest)],
+                    b_ssem.at[s, c, h], rb_sem.at[me, h], onward(s))
+
+    def fwd_b(s, t, h):
+        view = land_b[h].at[t, pl.ds(k * rest, rest)]
+        return rdma(view, view, b_ssem.at[s, t, h], rb_sem.at[t * 2 + k, h], onward(s))
+
+    def pair_b(t, h):
+        view = land_b[h].at[t, pl.ds(k * rest, rest)]
+        return rdma(view, view, b_psem.at[t, h], rb_sem.at[t * 2 + k, h], partner)
+
+    def got_b(t, kk, h):
+        view = land_b[h].at[t, pl.ds(kk * rest, rest)]
+        return rdma(view, view, b_psem.at[t, h], rb_sem.at[t * 2 + kk, h], partner)
+
+    def nat_copy(h):
+        return rdma(send[h].at[2], land_o[h].at[pl.ds(k * tok, tok)], o_ssem.at[h], rn_sem.at[h], partner)
+
+    def nat_here(h):
+        return pltpu.make_async_copy(send[h].at[2], land_o[h].at[pl.ds(k * tok, tok)], o_ssem.at[2 + h])
+
+    def wt_copy(j):
+        return rdma(wt_ref, wts.at[me], wt_ssem.at[j], wt_rsem.at[me], (stage, lax.rem(me + j, 2 * n)))
+
+    def wt_got(j):
+        src = lax.rem(me + j, 2 * n)
+        return rdma(wt_ref, wts.at[src], wt_ssem.at[j], wt_rsem.at[src], (stage, src))
+
+    pt_copy = rdma(pt_ref, pts, pt_ssem, pt_rsem, partner)
+    wp_copy = rdma(wgu.at[pl.ds(other * half_d, half_d)], wp, wp_ssem, wp_rsem, partner)
+
+    for s in range(2):
+
+        @pl.when(mirrored(s, c) < n - 1)
+        def _():
+            for h in range(2):
+                own_a(s, h).start()
+
+    for h in range(2):
+        nat_copy(h).start()
+        nat_here(h).start()
+    for j in range(1, 2 * n):
+        wt_copy(j).start()
+    wts[me] = wt_ref[...]
+    pt_copy.start()
+    for load in loads:
+        load.wait()
+    wp_copy.start()
+
+    def swap(slot, rows):
+        return rdma(gs.at[slot, pl.ds(0, rows)], gr.at[slot, pl.ds(0, rows)], g_ssem.at[slot], g_rsem.at[slot], partner)
+
+    def column(v):
+        return jnp.transpose(jnp.broadcast_to(v, (v.shape[1], v.shape[1])))[:, :1]
+
+    def terms(x_view, g_view, rows, slot, put_router):
+        step = 256 if (2 * hid) % 256 == 0 else 128
+
+        @pl.loop(0, 2 * hid // step)
+        def _(j):
+            cols = pl.ds(pl.multiple_of(j * step, step), step)
+            pre[pl.ds(0, rows), cols] = jnp.dot(x_view[...], wgu[:, cols], preferred_element_type=jnp.float32)
+
+        pre[pl.ds(0, rows), pl.ds(2 * hid, hid)] = lax.dot_general(
+            g_view[...], wd[...], NT, preferred_element_type=jnp.float32
+        )
+        chunk = 32
+
+        @pl.loop(0, rows // chunk)
+        def _(i):
+            at = pl.ds(pl.multiple_of(i * chunk, chunk), chunk)
+            gate_pre = pre[at, pl.ds(0, hid)]
+            up_pre = pre[at, pl.ds(hid, hid)]
+            back = pre[at, pl.ds(2 * hid, hid)]
+            squash = jax.nn.sigmoid(gate_pre)
+            activated = gate_pre * squash
+            hidden = (activated * up_pre).astype(jnp.bfloat16)
+            router = jnp.sum(hidden.astype(jnp.float32) * back, axis=1, keepdims=True)
+            slope = squash * (1.0 + gate_pre * (1.0 - squash))
+            gs[slot, at, pl.ds(0, hid)] = (back * up_pre * slope).astype(jnp.bfloat16)
+            gs[slot, at, pl.ds(hid, hid)] = (back * activated).astype(jnp.bfloat16)
+            pre[at, pl.ds(0, 128)] = jnp.broadcast_to(router, (chunk, 128))
+
+        swap(slot, rows).start()
+        put_router()
+
+    def products(rows, slot, weight):
+        step = 256 if half_d % 256 == 0 else 128
+
+        @pl.loop(0, half_d // step)
+        def _(j):
+            cols = pl.ds(pl.multiple_of(j * step, step), step)
+            mine = pl.ds(pl.multiple_of(k * half_d + j * step, step), step)
+            part[slot, pl.ds(0, rows), cols] = lax.dot_general(
+                gs[slot, pl.ds(0, rows)], wgu[mine, :], NT, preferred_element_type=jnp.float32
+            )
+
+        swap(slot, rows).wait()
+
+        @pl.loop(0, half_d // step)
+        def _(j):
+            cols = pl.ds(pl.multiple_of(j * step, step), step)
+            total = part[slot, pl.ds(0, rows), cols] + lax.dot_general(
+                gr[slot, pl.ds(0, rows)], wp[cols, :], NT, preferred_element_type=jnp.float32
+            )
+            part[slot, pl.ds(0, rows), cols] = total * weight
+
+    def row_weights(t, base, lo, size):
+        cols = [column(wts[t * 2 + kk, pl.ds(base + c, 1), :])[lo:lo + size] for kk in range(2)]
+        return jnp.concatenate(cols, axis=0)
+
+    for h in range(2):
+        rdma(send[h].at[2], land_o[h].at[pl.ds(other * tok, tok)], o_ssem.at[h], rn_sem.at[h], partner).wait_recv()
+        nat_here(h).wait()
+    for j in range(1, 2 * n):
+        wt_got(j).wait_recv()
+
+    def own_router():
+        for kk in range(2):
+            rl[c * 2 + kk] = pre[pl.ds(kk * tok, tok), pl.ds(0, 128)]
+
+    terms(xo, go, 2 * tok, n, own_router)
+    wp_copy.wait_recv()
+    products(2 * tok, n, row_weights(c, 2 * n, 0, tok))
+
+    def chain_a(s, t):
+        return rdma(ta.at[t], ca.at[s, t], ca_ssem.at[t], ca_rsem.at[s, t], backward(s))
+
+    def chain_b(s, t):
+        return rdma(tb.at[t], cb.at[s, t], cb_ssem.at[t], cb_rsem.at[s, t], backward(s))
+
+    def real(s, chip):
+        return chip if s == 0 else n - 1 - chip
+
+    def chain_step(at):
+        for s in range(2):
+            here = mirrored(s, c)
+            target = 2 * (n - 1) - here - at
+            t = real(s, target)
+
+            @pl.when((target >= 0) & (target < here))
+            def _():
+                @pl.when(here < n - 1)
+                def _():
+                    chain_a(s, t).wait_recv()
+                    ta[t] = (part[t, pl.ds(0, 2 * cap)] + ca[s, t].astype(jnp.float32)).astype(jnp.bfloat16)
+
+                @pl.when(here == n - 1)
+                def _():
+                    ta[t] = part[t, pl.ds(0, 2 * cap)].astype(jnp.bfloat16)
+
+                chain_a(s, t).start()
+
+    @pl.loop(1, n)
+    def _(d):
+        for s in range(2):
+            here = mirrored(s, c)
+            t = real(s, here - d)
+
+            @pl.when(here >= d)
+            def _():
+                for h in range(2):
+                    got_a(t, k, h).wait_recv()
+
+                    @pl.when(here < n - 1)
+                    def _():
+                        fwd_a(s, t, h).start()
+
+                    pair_a(t, h).start()
+
+        for s in range(2):
+            here = mirrored(s, c)
+
+            @pl.when((here < n - 2) & (d == jnp.maximum(here, 1)))
+            def _():
+                for h in range(2):
+                    own_b(s, h).start()
+
+        @pl.loop(0, 2)
+        def _(side):
+            t = jnp.where(side == 0, c - d, c + d)
+
+            @pl.when((t >= 0) & (t < n))
+            def _():
+                for h in range(2):
+                    got_a(t, other, h).wait_recv()
+
+                def put_router():
+                    for kk in range(2):
+                        rl[t * 2 + kk, pl.ds(0, cap)] = pre[pl.ds(kk * cap, cap), pl.ds(0, 128)]
+
+                terms(xa.at[t], ga.at[t], 2 * cap, t, put_router)
+                products(2 * cap, t, row_weights(t, side * n, 0, cap))
+
+        for s in range(2):
+            here = mirrored(s, c)
+            back = jnp.where(here < n - 2, d, d - 1)
+            t = real(s, here - back)
+
+            @pl.when((here >= back) & (back > 0) & (here < n - 1))
+            def _():
+                for h in range(2):
+                    got_b(t, k, h).wait_recv()
+
+                    @pl.when(here < n - 2)
+                    def _():
+                        fwd_b(s, t, h).start()
+
+                    pair_b(t, h).start()
+
+        chain_step(d)
+
+    inner = (c > 0) & (c < n - 1)
+
+    @pl.when(inner)
+    def _():
+        for j in range(1, n):
+            t = lax.rem(c + j, n)
+            for h in range(2):
+                got_b(t, other, h).wait_recv()
+
+        def put_router():
+            @pl.loop(0, n)
+            def _(t):
+                @pl.when(t != c)
+                def _():
+                    for kk in range(2):
+                        rl[t * 2 + kk, pl.ds(cap, rest)] = pre[
+                            pl.ds(pl.multiple_of(t * 2 * rest + kk * rest, rest), rest), pl.ds(0, 128)]
+
+        rows_b = n * 2 * rest
+        terms(xb.reshape(rows_b, xb.shape[2]), gb.reshape(rows_b, gb.shape[2]), rows_b, n + 1, put_router)
+        weights = [row_weights(t, jnp.where(t < c, 0, n), cap, rest) for t in range(n)]
+        products(rows_b, n + 1, jnp.concatenate(weights, axis=0))
+
+    def chain_step_b(here_at):
+        for s in range(2):
+            here = mirrored(s, c)
+
+            @pl.when(here == here_at)
+            def _():
+                for target in range(here_at):
+                    t = real(s, target)
+                    mine = part[n + 1, pl.ds(t * 2 * rest, 2 * rest)]
+                    if here_at < n - 2:
+                        chain_b(s, t).wait_recv()
+                        mine = mine + cb[s, t].astype(jnp.float32)
+                    tb[t] = mine.astype(jnp.bfloat16)
+                    chain_b(s, t).start()
+
+    for at in range(n, 2 * (n - 1)):
+        chain_step(at)
+        here_at = 2 * (n - 1) - at
+        if 0 < here_at <= n - 2:
+            chain_step_b(here_at)
+
+    def rr_copy(j):
+        dst = lax.rem(me + j, 2 * n)
+        return rdma(rs.at[dst], rr_ref.at[me], rr_ssem.at[j], rr_rsem.at[me], (stage, dst))
+
+    def rr_got(j):
+        src = lax.rem(me + j, 2 * n)
+        return rdma(rs.at[src], rr_ref.at[src], rr_ssem.at[j], rr_rsem.at[src], (stage, src))
+
+    @pl.loop(0, 2 * n)
+    def _(src):
+        rs[src] = jnp.transpose(rl[src])[:8]
+
+    for j in range(1, 2 * n):
+        rr_copy(j).start()
+    rr_ref[me] = rs[me]
+
+    pt_copy.wait_recv()
+
+    def place(s, rows_b):
+        for kk in range(2):
+            top = ca[s, c, pl.ds(kk * cap, cap)]
+            low = cb[s, c, pl.ds(kk * rest, rest)] if rows_b else jnp.zeros((rest, half_d), jnp.bfloat16)
+            spread = jnp.where(kk == k, pt_ref[s], pts[s])
+            at = pl.ds(kk * tok, tok)
+            part[n, at] += jnp.dot(spread, jnp.concatenate([top, low], axis=0), preferred_element_type=jnp.float32)
+
+    for s in range(2):
+        here = mirrored(s, c)
+
+        @pl.when(here < n - 1)
+        def _():
+            chain_a(s, c).wait_recv()
+
+        @pl.when(here < n - 2)
+        def _():
+            chain_b(s, c).wait_recv()
+            place(s, True)
+
+        @pl.when(here == n - 2)
+        def _():
+            place(s, False)
+
+    def last(kk):
+        return rdma(fin.at[kk], out_ref.at[:, pl.ds(k * half_d, half_d)], f_ssem.at[kk], f_rsem.at[k],
+                    (stage - 1, c * 2 + kk))
+
+    @pl.when(stage > 0)
+    def _():
+        for kk in range(2):
+            fin[kk] = part[n, pl.ds(kk * tok, tok)].astype(jnp.bfloat16)
+            last(kk).start()
+
+    @pl.when(stage == stages - 1)
+    def _():
+        out_ref[...] = jnp.zeros_like(out_ref)
+
+    @pl.when(stage < stages - 1)
+    def _():
+        for kk in range(2):
+            rdma(fin.at[kk], out_ref.at[:, pl.ds(kk * half_d, half_d)], f_ssem.at[kk], f_rsem.at[kk],
+                 (stage, me)).wait_recv()
+
+    @pl.when(stage > 0)
+    def _():
+        for kk in range(2):
+            last(kk).wait_send()
+
+    for j in range(1, 2 * n):
+        rr_got(j).wait_recv()
+        rr_copy(j).wait_send()
+        wt_copy(j).wait_send()
+    pt_copy.wait_send()
+    wp_copy.wait_send()
+    for h in range(2):
+        nat_copy(h).wait_send()
+    for s in range(2):
+        here = mirrored(s, c)
+        for h in range(2):
+
+            @pl.when(here < n - 1)
+            def _():
+                own_a(s, h).wait_send()
+
+            @pl.when(here < n - 2)
+            def _():
+                own_b(s, h).wait_send()
+
+        for d in range(1, n):
+            t = real(s, here - d)
+
+            @pl.when(here >= d)
+            def _():
+                chain_a(s, t).wait_send()
+                for h in range(2):
+                    pair_a(t, h).wait_send()
+
+                    @pl.when(here < n - 1)
+                    def _():
+                        fwd_a(s, t, h).wait_send()
+                        pair_b(t, h).wait_send()
+
+                    @pl.when(here < n - 2)
+                    def _():
+                        fwd_b(s, t, h).wait_send()
+
+                @pl.when(here < n - 1)
+                def _():
+                    chain_b(s, t).wait_send()
+
+
+def line_local(activations, out_grad, expert_ids, gate_values, w_gate, w_up, w_down):
+    x, g, ids, gates = activations[0], out_grad[0], expert_ids[0], gate_values[0]
+    n = lax.axis_size("expert") // 2
+    tok, feat = x.shape
+    hid = w_down.shape[1]
+    cap = tok * 3 // 4
+    rest = tok - cap
+    half_d = feat // 2
+    c = lax.axis_index("expert") // 2
+    owners = jnp.arange(n, dtype=jnp.int32)
+    routed = ids[:, :, None] == owners
+    weights = jnp.sum(jnp.where(routed, gates[:, :, None], 0.0), axis=1)
+    named = jnp.any(routed, axis=1)
+    order = jnp.arange(tok, dtype=jnp.int32)
+    before = order[None, :] < order[:, None]
+
+    def places(first):
+        ahead = jnp.sum((before & first[None, :]).astype(jnp.int32), axis=1)
+        behind = jnp.sum((before & ~first[None, :]).astype(jnp.int32), axis=1)
+        return jnp.where(first, ahead, jnp.sum(first.astype(jnp.int32)) + behind)
+
+    spots = jnp.stack([places(named[:, n - 1]), places(named[:, 0]), order])
+    moves = spots[:, None, :] == order[None, :, None]
+    moves16 = moves.astype(jnp.bfloat16)
+    flat = moves16.reshape(3 * tok, tok)
+    send_x = jnp.dot(flat, x, preferred_element_type=jnp.float32).astype(x.dtype).reshape(3, tok, feat)
+    send_g = jnp.dot(flat, g, preferred_element_type=jnp.float32).astype(g.dtype).reshape(3, tok, feat)
+    wt = jnp.sum(jnp.where(moves[:, None], weights.T[None, :, None, :], 0.0), axis=3).reshape(3 * n, tok)
+    wt = jnp.pad(wt, ((0, -(3 * n) % 8), (0, 0)))
+    pt = jnp.swapaxes(moves16[:2], 1, 2)
+    bf, f32 = jnp.bfloat16, jnp.float32
+    vmem, dma = pltpu.VMEM, pltpu.SemaphoreType.DMA
+    big = max(2 * tok, 2 * n * rest)
+    scratch = [
+        vmem((n, 2 * cap, feat), bf), vmem((n, 2 * cap, feat), bf),
+        vmem((n, 2 * rest, feat), bf), vmem((n, 2 * rest, feat), bf),
+        vmem((2 * tok, feat), bf), vmem((2 * tok, feat), bf),
+        vmem((feat, 2 * hid), bf), vmem((hid, feat), bf), vmem((half_d, 2 * hid), bf),
+        vmem((big, 3 * hid), f32),
+        vmem((n + 2, big, 2 * hid), bf), vmem((n + 2, big, 2 * hid), bf),
+        vmem((n + 2, big, half_d), f32),
+        vmem((2, n, 2 * cap, half_d), bf), vmem((2, n, 2 * rest, half_d), bf),
+        vmem((n, 2 * cap, half_d), bf), vmem((n, 2 * rest, half_d), bf),
+        vmem((2, tok, half_d), bf),
+        vmem((2 * n,) + wt.shape, f32), vmem((2, tok, tok), bf),
+        vmem((2 * n, tok, 128), f32), vmem((2 * n, 8, tok), f32),
+        dma((3,)), dma((4,)), dma((2,)), dma((2, n, 2)), dma((n, 2)), dma((2 * n, 2)),
+        dma((2, n, 2)), dma((n, 2)), dma((2 * n, 2)), dma((2 * n,)), dma((2 * n,)),
+        dma, dma, dma, dma, dma((n + 2,)), dma((n + 2,)), dma((n,)), dma((2, n)), dma((n,)), dma((2, n)),
+        dma((2 * n,)), dma((2 * n,)), dma((2,)), dma((2,)),
+    ]
+    in_vmem = pl.BlockSpec(memory_space=pltpu.VMEM)
+    passed, rr = pl.pallas_call(
+        functools.partial(line_kernel, n, cap),
+        out_shape=(jax.ShapeDtypeStruct((tok, feat), bf), jax.ShapeDtypeStruct((2 * n, 8, tok), f32)),
+        in_specs=[in_vmem] * 4 + [pl.BlockSpec(memory_space=pl.ANY)] * 3,
+        out_specs=(in_vmem, in_vmem),
+        scratch_shapes=scratch,
+        compiler_params=pltpu.CompilerParams(
+            collective_id=0, has_side_effects=True, vmem_limit_bytes=60 * 1024 * 1024
+        ),
+        name="line",
+    )(send_x, send_g, wt, pt, w_gate[0], w_up[0], w_down[0])
+    router = jnp.sum(rr[:, 0].reshape(n, 2, tok), axis=1)
+    spot = jnp.where(ids > c, spots[0][:, None], jnp.where(ids < c, spots[1][:, None], order[:, None]))
+    hit = routed[:, :, :, None] & (spot[:, :, None, None] == order)
+    entry = jnp.sum(jnp.where(hit, router, 0.0), axis=(2, 3))
+    return (passed[None], entry[None])
+
+
+def local(*args):
+    n = lax.axis_size("expert") // 2
+    tok, feat = args[0].shape[1:]
+    hid = args[6].shape[1]
+    scratch = 2 * n * tok * (feat * 7 + hid * 8) + 6 * feat * hid * 2
+    fits = scratch < 40 * 2**20 and tok == 128 and feat % 256 == 0 and hid % 128 == 0
+    if fits and n >= 4 and args[2].shape[2] * 2 == n:
+        return line_local(*args)
+    return routed_local(*args)
+
+
 def solution(mesh):
     return jax.shard_map(
         local,

time: 351 us -> 161 us (0.46)
  waiting for transfers between devices: 255 us -> 0 us
  Pallas kernels: 0 us -> 146 us
  local copies, waits for them, and re-layouts: 32.9 us -> 3.52 us
  starting transfers between devices: 18.7 us -> 0 us
  matrix products: 20.5 us -> 3.88 us
  blocking collectives: 8.21 us -> 0 us
  other arithmetic: 12.8 us -> 6.33 us
    all_to_all x3 -> x0, waiting for transfers between devices: 250 us -> none  [the longest x1 87.4 us: local(): lax.all_to_all(route_part.astype(jnp.bfloat16), 'expert', split_axis=0, c...]
    pallas_call x0 -> x1, Pallas kernels: none -> 146 us  [line_local(): pl.pallas_call(functools.partial(line_kernel, n, cap), out_shape=(jax.Sha...]
    all_to_all x3 -> x0, starting transfers between devices: 17.4 us -> none  [the longest x1 6.5 us: local(): lax.all_to_all(jnp.repeat(send_in, 2, axis=0), 'expert', split_axis=0, co...]
    dot_general x5 -> x2, matrix products: 20.5 us -> 3.88 us  [the longest x1 1.94 us: line_local(): jnp.dot(flat, x, preferred_element_type=jnp.float32).astype(x.dtype)]
    gather x4 -> x0, local copies, waits for them, and re-layouts: 14.8 us -> none  [the longest x1 6.23 us: local(): entry_route = route_sum.reshape(-1, feat_width)[slot_index]]
    reduce_sum x4 -> x7, other arithmetic: 10.8 us -> 2.08 us  [the longest x1 0.85 us: line_local(): entry = jnp.sum(jnp.where(hit, router, 0.0), axis=(2, 3))]
    all_to_all x1 -> x0, blocking collectives: 8.21 us -> none  [local(): lax.all_to_all(router_part.astype(jnp.bfloat16), 'expert', split_axis=0,...]
    broadcast_in_dim x2 -> x0, local copies, waits for them, and re-layouts: 7.56 us -> none  [the longest x1 3.78 us: local(): jnp.repeat(send_grad, 2, axis=0)]
  transfers between devices with their start and end apart: 4 -> 0, of which waited for: 4 -> 0; matrix products, arithmetic and copies ran while one was open for 4% -> 0% of each run, Pallas kernels for 0% -> 0%
where the time goes in v1:
time: 161 us
  Pallas kernels  146 us (91%)
  other arithmetic  6.33 us (4%)
  matrix products  3.88 us (2%)
  local copies, waits for them, and re-layouts  3.52 us (2%)
    pallas_call x1, Pallas kernels, line_local(): pl.pallas_call(functools.partial(line_kernel, n, cap), out_shape=(jax.Sha...  146 us

profile of v1, /device:TPU:1, one launch (start us, length us, event | category | flops | bytes accessed | tf_op | source)
XLA Modules:
  0.0 160.8 jit_solution(6411702900019635153)
XLA Ops:
  0.6 0.0 copy-start
  0.6 0.0 copy-start.1
  0.7 0.8 iota_compare_fusion.3
  1.5 0.1 convert_reduce_fusion
  1.6 0.1 convert_reduce_fusion.1
  1.7 0.7 convert_reduce_fusion.5
  2.4 1.3 bitcast_select_fusion.1
  3.7 0.1 iota_compare_fusion
  3.8 0.1 copy.18
  4.0 0.0 copy-done
  4.0 1.9 %convolution_convert_fusion.1 = bf16[384,2560]{1,0:T(8,128)(2,1)} fusion(pred[384,128]{1,0:T(8,128)(4,1)S(1)} %bitcast.68, bf16[1,128,2560]{2,1,0:T(8,128)(2,1)S(1)} %copy-done), kind=kOutput, calls=%fused_computation.1 | convolution fusion | flops 252641280 | bytes 2670592 | tf_op jit(solution)/shard_map/dot_general | solution.py:572
  5.9 0.0 copy-start.2
  5.9 0.0 copy-start.3
  5.9 0.0 copy-done.1
  5.9 1.9 %convolution_convert_fusion = bf16[384,2560]{1,0:T(8,128)(2,1)} fusion(pred[384,128]{1,0:T(8,128)(4,1)S(1)} %bitcast.69, bf16[1,128,2560]{2,1,0:T(8,128)(2,1)S(1)} %copy-done.1), kind=kOutput, calls=%fused_computation | convolution fusion | flops 252641280 | bytes 2670592 | tf_op jit(solution)/shard_map/dot_general | solution.py:573
  7.9 0.0 copy-done.2
  7.9 0.0 copy-done.3
  7.9 0.3 select_reduce_fusion
  8.2 0.6 pad.4.wt_ref
  8.8 0.7 fusion.2.pt_ref
  9.5 146.4 %line.1 = (bf16[128,2560]{1,0:T(8,128)(2,1)}, f32[8,8,128]{2,1,0:T(8,128)}) custom-call(bf16[3,128,2560]{2,1,0:T(8,128)(2,1)} %bitcast.63, bf16[3,128,2560]{2,1,0:T(8,128)(2,1)} %bitcast.64, f32[16,128]{1,0:T(8,128)} %pad.4.wt_ref, bf16[2,128,128]{2,1,0:T(8,128)(2,1)} %fusion.2.pt_ref, bf16[2560,384]{1,0:T(8,128)(2,1)} %bitcast.65, ...), custom_call_target="tpu_custom_call" | custom-call | tf_op jit(solution)/shard_map/line/pallas_call | solution.py:599
  155.8 0.8 slice.16
  156.6 1.3 fusion.8
  157.9 0.1 iota_compare_fusion.1
  158.0 0.9 select_reduce_fusion.1
  158.9 2.0 %copy.22 = bf16[1,128,2560]{2,1,0:T(8,128)(2,1)} copy(bf16[1,128,2560]{2,1,0:T(8,128)(2,1)} %bitcast.70) | data formatting | bytes 1310720
  (8 shorter events, 0.1 us)
Async XLA Ops:
  0.6 3.4 %copy-start = (bf16[1,128,2560]{2,1,0:T(8,128)(2,1)S(1)}, bf16[1,128,2560]{2,1,0:T(8,128)(2,1)}, u32[]{:S(2)}) copy-start(bf16[1,128,2560]{2,1,0:T(8,128)(2,1)} %param.7) | copy-start | bytes 1966084
  0.6 5.3 %copy-start.1 = (bf16[1,128,2560]{2,1,0:T(8,128)(2,1)S(1)}, bf16[1,128,2560]{2,1,0:T(8,128)(2,1)}, u32[]{:S(2)}) copy-start(bf16[1,128,2560]{2,1,0:T(8,128)(2,1)} %param.8) | copy-start | bytes 1966084
  5.9 1.9 %copy-start.2 = (s32[1,128,2]{1,2,0:T(2,128)S(1)}, s32[1,128,2]{1,2,0:T(2,128)}, u32[]{:S(2)}) copy-start(s32[1,128,2]{1,2,0:T(2,128)} %param.9) | copy-start | bytes 3076
  5.9 1.9 %copy-start.3 = (f32[1,128,2]{1,2,0:T(2,128)S(1)}, f32[1,128,2]{1,2,0:T(2,128)}, u32[]{:S(2)}) copy-start(f32[1,128,2]{1,2,0:T(2,128)} %param.10) | copy-start | bytes 3076

commit v2 on v1

--- a/solution.py
+++ b/solution.py
@@ -104,8 +104,8 @@
 
 
 def line_kernel(
-    n, cap, sx_ref, sg_ref, wt_ref, pt_ref, wg_hbm, wu_hbm, wd_hbm, out_ref, rr_ref,
-    xa, ga, xb, gb, xo, go, wgu, wd, wp, pre, gs, gr, part, ca, cb, ta, tb, fin, wts, pts, rl, rs,
+    n, cap, x_ref, g_ref, wt_ref, spot_ref, wg_hbm, wu_hbm, wd_hbm, out_ref, rr_ref,
+    sx, sg, pt, xa, ga, xb, gb, xo, go, wgu, wd, wp, pre, gs, gr, part, ca, cb, ta, tb, fin, wts, pts, rl, rs,
     w_sem, o_ssem, rn_sem, a_ssem, a_psem, ra_sem, b_ssem, b_psem, rb_sem, wt_ssem, wt_rsem,
     pt_ssem, pt_rsem, wp_ssem, wp_rsem, g_ssem, g_rsem, ca_ssem, ca_rsem, cb_ssem, cb_rsem,
     rr_ssem, rr_rsem, f_ssem, f_rsem,
@@ -115,12 +115,12 @@
     stages = lax.axis_size("pipe")
     c, k = lax.div(me, 2), lax.rem(me, 2)
     other = 1 - k
-    tok = sx_ref.shape[1]
+    tok = x_ref.shape[0]
     rest = tok - cap
     hid = wd.shape[0]
     half_d = wp.shape[0]
     partner = (stage, c * 2 + other)
-    send, land_a, land_b, land_o = (sx_ref, sg_ref), (xa, ga), (xb, gb), (xo, go)
+    rows_in, send, land_a, land_b, land_o = (x_ref, g_ref), (sx, sg), (xa, ga), (xb, gb), (xo, go)
 
     def rdma(src, dst, ssem, rsem, dev):
         return pltpu.make_async_remote_copy(
@@ -135,6 +135,14 @@
     for load in loads:
         load.start()
     rl[...] = jnp.zeros_like(rl)
+    order = lax.broadcasted_iota(jnp.int32, (tok, tok), 0)
+    for s in range(2):
+        move = jnp.where(jnp.broadcast_to(spot_ref[pl.ds(s, 1), :], (tok, tok)) == order, 1.0, 0.0)
+        pt[s] = jnp.transpose(move).astype(jnp.bfloat16)
+        for h in range(2):
+            send[h][s] = jnp.dot(
+                move.astype(jnp.bfloat16), rows_in[h][...], preferred_element_type=jnp.float32
+            ).astype(jnp.bfloat16)
 
     barrier = pltpu.get_barrier_semaphore()
     for j in range(1, 2 * n):
@@ -194,10 +202,10 @@
         return rdma(view, view, b_psem.at[t, h], rb_sem.at[t * 2 + kk, h], partner)
 
     def nat_copy(h):
-        return rdma(send[h].at[2], land_o[h].at[pl.ds(k * tok, tok)], o_ssem.at[h], rn_sem.at[h], partner)
+        return rdma(rows_in[h], land_o[h].at[pl.ds(k * tok, tok)], o_ssem.at[h], rn_sem.at[h], partner)
 
     def nat_here(h):
-        return pltpu.make_async_copy(send[h].at[2], land_o[h].at[pl.ds(k * tok, tok)], o_ssem.at[2 + h])
+        return pltpu.make_async_copy(rows_in[h], land_o[h].at[pl.ds(k * tok, tok)], o_ssem.at[2 + h])
 
     def wt_copy(j):
         return rdma(wt_ref, wts.at[me], wt_ssem.at[j], wt_rsem.at[me], (stage, lax.rem(me + j, 2 * n)))
@@ -206,7 +214,7 @@
         src = lax.rem(me + j, 2 * n)
         return rdma(wt_ref, wts.at[src], wt_ssem.at[j], wt_rsem.at[src], (stage, src))
 
-    pt_copy = rdma(pt_ref, pts, pt_ssem, pt_rsem, partner)
+    pt_copy = rdma(pt, pts, pt_ssem, pt_rsem, partner)
     wp_copy = rdma(wgu.at[pl.ds(other * half_d, half_d)], wp, wp_ssem, wp_rsem, partner)
 
     for s in range(2):
@@ -290,7 +298,7 @@
         return jnp.concatenate(cols, axis=0)
 
     for h in range(2):
-        rdma(send[h].at[2], land_o[h].at[pl.ds(other * tok, tok)], o_ssem.at[h], rn_sem.at[h], partner).wait_recv()
+        rdma(rows_in[h], land_o[h].at[pl.ds(other * tok, tok)], o_ssem.at[h], rn_sem.at[h], partner).wait_recv()
         nat_here(h).wait()
     for j in range(1, 2 * n):
         wt_got(j).wait_recv()
@@ -303,8 +311,11 @@
     wp_copy.wait_recv()
     products(2 * tok, n, row_weights(c, 2 * n, 0, tok))
 
-    def chain_a(s, t):
-        return rdma(ta.at[t], ca.at[s, t], ca_ssem.at[t], ca_rsem.at[s, t], backward(s))
+    quarter = cap // 2
+
+    def chain_a(s, t, q):
+        at = pl.ds(q * quarter, quarter)
+        return rdma(ta.at[t, at], ca.at[s, t, at], ca_ssem.at[t, q], ca_rsem.at[s, t, q], backward(s))
 
     def chain_b(s, t):
         return rdma(tb.at[t], cb.at[s, t], cb_ssem.at[t], cb_rsem.at[s, t], backward(s))
@@ -320,16 +331,19 @@
 
             @pl.when((target >= 0) & (target < here))
             def _():
-                @pl.when(here < n - 1)
-                def _():
-                    chain_a(s, t).wait_recv()
-                    ta[t] = (part[t, pl.ds(0, 2 * cap)] + ca[s, t].astype(jnp.float32)).astype(jnp.bfloat16)
-
-                @pl.when(here == n - 1)
-                def _():
-                    ta[t] = part[t, pl.ds(0, 2 * cap)].astype(jnp.bfloat16)
-
-                chain_a(s, t).start()
+                for q in range(4):
+                    at_q = pl.ds(q * quarter, quarter)
+
+                    @pl.when(here < n - 1)
+                    def _():
+                        chain_a(s, t, q).wait_recv()
+                        ta[t, at_q] = (part[t, at_q] + ca[s, t, at_q].astype(jnp.float32)).astype(jnp.bfloat16)
+
+                    @pl.when(here == n - 1)
+                    def _():
+                        ta[t, at_q] = part[t, at_q].astype(jnp.bfloat16)
+
+                    chain_a(s, t, q).start()
 
     @pl.loop(1, n)
     def _(d):
@@ -428,11 +442,10 @@
                     tb[t] = mine.astype(jnp.bfloat16)
                     chain_b(s, t).start()
 
+    for here_at in range(n - 2, 0, -1):
+        chain_step_b(here_at)
     for at in range(n, 2 * (n - 1)):
         chain_step(at)
-        here_at = 2 * (n - 1) - at
-        if 0 < here_at <= n - 2:
-            chain_step_b(here_at)
 
     def rr_copy(j):
         dst = lax.rem(me + j, 2 * n)
@@ -452,37 +465,43 @@
 
     pt_copy.wait_recv()
 
-    def place(s, rows_b):
-        for kk in range(2):
-            top = ca[s, c, pl.ds(kk * cap, cap)]
-            low = cb[s, c, pl.ds(kk * rest, rest)] if rows_b else jnp.zeros((rest, half_d), jnp.bfloat16)
-            spread = jnp.where(kk == k, pt_ref[s], pts[s])
-            at = pl.ds(kk * tok, tok)
-            part[n, at] += jnp.dot(spread, jnp.concatenate([top, low], axis=0), preferred_element_type=jnp.float32)
-
-    for s in range(2):
-        here = mirrored(s, c)
-
-        @pl.when(here < n - 1)
-        def _():
-            chain_a(s, c).wait_recv()
-
-        @pl.when(here < n - 2)
-        def _():
-            chain_b(s, c).wait_recv()
-            place(s, True)
-
-        @pl.when(here == n - 2)
-        def _():
-            place(s, False)
+    def place(s, kk, rows_b):
+        top = ca[s, c, pl.ds(kk * cap, cap)]
+        low = cb[s, c, pl.ds(kk * rest, rest)] if rows_b else jnp.zeros((rest, half_d), jnp.bfloat16)
+        spread = jnp.where(kk == k, pt[s], pts[s])
+        part[n, pl.ds(kk * tok, tok)] += jnp.dot(
+            spread, jnp.concatenate([top, low], axis=0), preferred_element_type=jnp.float32
+        )
 
     def last(kk):
         return rdma(fin.at[kk], out_ref.at[:, pl.ds(k * half_d, half_d)], f_ssem.at[kk], f_rsem.at[k],
                     (stage - 1, c * 2 + kk))
 
-    @pl.when(stage > 0)
-    def _():
-        for kk in range(2):
+    for s in range(2):
+
+        @pl.when(mirrored(s, c) < n - 2)
+        def _():
+            chain_b(s, c).wait_recv()
+
+    for kk in range(2):
+        for s in range(2):
+            here = mirrored(s, c)
+
+            @pl.when(here < n - 1)
+            def _():
+                for q in range(2):
+                    chain_a(s, c, 2 * kk + q).wait_recv()
+
+            @pl.when(here < n - 2)
+            def _():
+                place(s, kk, True)
+
+            @pl.when(here == n - 2)
+            def _():
+                place(s, kk, False)
+
+        @pl.when(stage > 0)
+        def _():
             fin[kk] = part[n, pl.ds(kk * tok, tok)].astype(jnp.bfloat16)
             last(kk).start()
 
@@ -526,7 +545,8 @@
 
             @pl.when(here >= d)
             def _():
-                chain_a(s, t).wait_send()
+                for q in range(4):
+                    chain_a(s, t, q).wait_send()
                 for h in range(2):
                     pair_a(t, h).wait_send()
 
@@ -567,17 +587,13 @@
 
     spots = jnp.stack([places(named[:, n - 1]), places(named[:, 0]), order])
     moves = spots[:, None, :] == order[None, :, None]
-    moves16 = moves.astype(jnp.bfloat16)
-    flat = moves16.reshape(3 * tok, tok)
-    send_x = jnp.dot(flat, x, preferred_element_type=jnp.float32).astype(x.dtype).reshape(3, tok, feat)
-    send_g = jnp.dot(flat, g, preferred_element_type=jnp.float32).astype(g.dtype).reshape(3, tok, feat)
     wt = jnp.sum(jnp.where(moves[:, None], weights.T[None, :, None, :], 0.0), axis=3).reshape(3 * n, tok)
     wt = jnp.pad(wt, ((0, -(3 * n) % 8), (0, 0)))
-    pt = jnp.swapaxes(moves16[:2], 1, 2)
     bf, f32 = jnp.bfloat16, jnp.float32
     vmem, dma = pltpu.VMEM, pltpu.SemaphoreType.DMA
     big = max(2 * tok, 2 * n * rest)
     scratch = [
+        vmem((2, tok, feat), bf), vmem((2, tok, feat), bf), vmem((2, tok, tok), bf),
         vmem((n, 2 * cap, feat), bf), vmem((n, 2 * cap, feat), bf),
         vmem((n, 2 * rest, feat), bf), vmem((n, 2 * rest, feat), bf),
         vmem((2 * tok, feat), bf), vmem((2 * tok, feat), bf),
@@ -592,7 +608,7 @@
         vmem((2 * n, tok, 128), f32), vmem((2 * n, 8, tok), f32),
         dma((3,)), dma((4,)), dma((2,)), dma((2, n, 2)), dma((n, 2)), dma((2 * n, 2)),
         dma((2, n, 2)), dma((n, 2)), dma((2 * n, 2)), dma((2 * n,)), dma((2 * n,)),
-        dma, dma, dma, dma, dma((n + 2,)), dma((n + 2,)), dma((n,)), dma((2, n)), dma((n,)), dma((2, n)),
+        dma, dma, dma, dma, dma((n + 2,)), dma((n + 2,)), dma((n, 4)), dma((2, n, 4)), dma((n,)), dma((2, n)),
         dma((2 * n,)), dma((2 * n,)), dma((2,)), dma((2,)),
     ]
     in_vmem = pl.BlockSpec(memory_space=pltpu.VMEM)
@@ -606,7 +622,7 @@
             collective_id=0, has_side_effects=True, vmem_limit_bytes=60 * 1024 * 1024
         ),
         name="line",
-    )(send_x, send_g, wt, pt, w_gate[0], w_up[0], w_down[0])
+    )(x, g, wt, spots, w_gate[0], w_up[0], w_down[0])
     router = jnp.sum(rr[:, 0].reshape(n, 2, tok), axis=1)
     spot = jnp.where(ids > c, spots[0][:, None], jnp.where(ids < c, spots[1][:, None], order[:, None]))
     hit = routed[:, :, :, None] & (spot[:, :, None, None] == order)

time: 161 us -> 138 us (0.86)
  Pallas kernels: 146 us -> 127 us
  matrix products: 3.88 us -> 0 us
    pallas_call x1, Pallas kernels: 146 us -> 127 us  [line_local(): pl.pallas_call(functools.partial(line_kernel, n, cap), out_shape=(jax.Sha...]
    dot_general x2 -> x0, matrix products: 3.88 us -> none  [the longest x1 1.94 us: line_local(): jnp.dot(flat, x, preferred_element_type=jnp.float32).astype(x.dtype)]
where the time goes in v2:
time: 138 us; the launch traced here: 137 us
  Pallas kernels  127 us (92%)
  other arithmetic  6.04 us (4%)
  local copies, waits for them, and re-layouts  3.37 us (2%)
    pallas_call x1, Pallas kernels, line_local(): pl.pallas_call(functools.partial(line_kernel, n, cap), out_shape=(jax.Sha...  127 us

profile of v2, /device:TPU:1, one launch (start us, length us, event | category | flops | bytes accessed | tf_op | source)
XLA Modules:
  0.0 137.2 jit_solution(2380283434236099828)
XLA Ops:
  0.6 0.7 iota_compare_fusion.3
  1.3 0.1 convert_reduce_fusion
  1.5 0.1 convert_reduce_fusion.1
  1.6 0.7 convert_reduce_fusion.5
  2.2 1.2 bitcast_select_fusion.1
  3.5 0.0 copy-start
  3.5 0.7 select_reduce_fusion.2
  4.2 0.3 select_reduce_fusion
  4.5 0.6 pad.4.wt_ref
  5.2 0.0 copy-done
  5.2 0.0 copy-start.1
  5.2 127.0 %line.1 = (bf16[128,2560]{1,0:T(8,128)(2,1)}, f32[8,8,128]{2,1,0:T(8,128)}) custom-call(bf16[128,2560]{1,0:T(8,128)(2,1)} %bitcast.55, bf16[128,2560]{1,0:T(8,128)(2,1)} %bitcast.56, f32[16,128]{1,0:T(8,128)} %pad.4.wt_ref, s32[3,128]{1,0:T(4,128)} %copy-done, bf16[2560,384]{1,0:T(8,128)(2,1)} %bitcast.52, bf16[2560,384]{1,0:T(8,128)(2,1)} %bitcast.53, ...), custom_call_target="tpu_custom_call" | custom-call | tf_op jit(solution)/shard_map/line/pallas_call | solution.py:615
  132.2 0.8 slice.11
  133.0 1.2 fusion.5
  134.2 0.0 copy-done.1
  134.3 0.1 iota_compare_fusion.1
  134.4 0.9 select_reduce_fusion.1
  135.2 2.0 %copy.13 = bf16[1,128,2560]{2,1,0:T(8,128)(2,1)} copy(bf16[1,128,2560]{2,1,0:T(8,128)(2,1)} %bitcast.57) | data formatting | bytes 1310720
  (8 shorter events, 0.1 us)
Async XLA Ops:
  3.5 1.7 %copy-start = (s32[3,128]{1,0:T(4,128)}, s32[3,128]{1,0:T(4,128)S(1)}, u32[]{:S(2)}) copy-start(s32[3,128]{1,0:T(4,128)S(1)} %pad_add_fusion.spot_ref) | copy-start | bytes 4612
  5.2 129.1 %copy-start.1 = (s32[1,128,2]{1,2,0:T(2,128)S(1)}, s32[1,128,2]{1,2,0:T(2,128)}, u32[]{:S(2)}) copy-start(s32[1,128,2]{1,2,0:T(2,128)} %param.9) | copy-start | bytes 3076
